TPU v7x, 32 devices: a whole 2x2x4 slice. The times are simulated.
32 devices in a mesh: grp: 4 (over y, x), dev: 8 (over z, core).
Axes of the slice: x: 2, y: 2, z: 4, core: 2. Of those that a mesh axis runs over, the one named last changes fastest.
Arguments:
- positions: bfloat16 [3, 131072], P(None, ('grp', 'dev')), may hold values from 0 to 1.5
- features: bfloat16 [131072, 128], P(('grp', 'dev')), may hold values from -6 to 6
- tile_first: int32 [256], P(('grp', 'dev')), may hold values from 0 to 31
- tile_second: int32 [256], P(('grp', 'dev')), may hold values from 0 to 127
- count_first: int32 [256], P(('grp', 'dev')), may hold values from 32 to 128
- count_second: int32 [256], P(('grp', 'dev')), may hold values from 32 to 128
- w_first: bfloat16 [128, 128], replicated, may hold values from -0.5 to 0.5
- w_second: bfloat16 [128, 128], replicated, may hold values from -0.5 to 0.5
- radial_weight: bfloat16 [16, 128], replicated, may hold values from -3 to 3
- mix_weight: bfloat16 [128, 128], replicated, may hold values from -0.5 to 0.5
- out_weight: float32 [128], replicated, may hold values from -1.5 to 1.5
Outputs:
- forces: float32 [3, 131072], P(None, ('grp', 'dev'))
All inputs are finite; a program needn't handle non-finite values.
Results may differ from a plain program's by a relative error of at most 0.0023.
Values may be sent and summed in bfloat16 or wider, within the bound.
No kernel may reach another device: no remote copies, remote signals or barrier semaphores. Data moves between devices by JAX's collectives and lax.ppermute only.
A program may use at most 64 MiB of HBM per device.

v0:
```python
import functools

import jax
import jax.numpy as jnp
from jax import lax
from jax.experimental import pallas as pl
from jax.experimental.pallas import tpu as pltpu
from jax.sharding import PartitionSpec as P

CELL = 128
NB = 16
UNIT = 8
UNITS = 2
ROWS = UNIT * UNITS
PACKED = CELL + 16
EARLY = 16
F32, BF = jnp.float32, jnp.bfloat16
LAST = (((1,), (1,)), ((), ()))
VMEM = pl.BlockSpec(memory_space=pltpu.VMEM)


def shifted(array, groups, members):
    n_grp, n_dev = lax.axis_size("grp"), lax.axis_size("dev")
    if groups == 0:
        return lax.ppermute(array, "dev", [(i, (i + members) % n_dev) for i in range(n_dev)])
    if members == 0:
        return lax.ppermute(array, "grp", [(i, (i + groups) % n_grp) for i in range(n_grp)])
    pairs = [
        (g * n_dev + d, (g + groups) % n_grp * n_dev + (d + members) % n_dev)
        for g in range(n_grp)
        for d in range(n_dev)
    ]
    return lax.ppermute(array, ("grp", "dev"), pairs)


def dot(a, b):
    return jnp.dot(a, b, preferred_element_type=F32)


def cell_at(ref, cell):
    return ref[pl.ds(pl.multiple_of(cell * CELL, CELL), CELL), :]


def place_at(ref, cell):
    return ref[:, pl.ds(pl.multiple_of(cell * CELL, CELL), CELL)]


def tall(places):
    return jnp.concatenate([places.astype(F32), jnp.zeros((5, CELL), F32)], axis=0)


def pack_kernel(wanted, _, own_f, own_p, side_f, side_p, out):
    cells = own_f.shape[0] // CELL
    for slot in range(wanted.shape[0]):
        block, cell = wanted[slot] // cells, wanted[slot] % cells

        def put(feats, places, slot=slot, cell=cell):
            base = slot * PACKED
            out[base : base + CELL, :] = cell_at(feats, cell)
            rows = jnp.concatenate([tall(place_at(places, cell)), jnp.zeros((8, CELL), F32)], axis=0)
            out[base + CELL : base + PACKED, :] = rows.astype(BF)

        pl.when(block == 2)(functools.partial(put, own_f, own_p))
        pl.when(block == 3)(functools.partial(put, side_f, side_p))


def tile_kernel(
    stage, first, second, live_a, live_b, own_f, own_p, *refs
):
    extra = (0, 3, 2)[stage]
    remote, refs = refs[:extra], refs[extra:]
    outs = (1, 2, 2)[stage]
    (w_a, w_b, radial, mix, out_w), refs = refs[:5], refs[5:]
    total, side = refs[0], refs[outs - 1]
    refs = refs[outs:]
    if stage == 0:
        given = (own_f, own_p, w_a, w_b, radial, mix, out_w)
        own_f, own_p, w_a, w_b, radial, mix, out_w = held = refs[-8:-1]
        copies = [pltpu.make_async_copy(*pair, refs[-1].at[k]) for k, pair in enumerate(zip(given, held))]
        for copy in copies:
            copy.start()
        for copy in copies:
            copy.wait()
        refs = refs[:-8]
    (
     flip, mix_t, mix_o, scale_o, last, onehot, proj_r, proj_l, dist, slope_sum, read_sum, fb, pa, pb, near_rows, half_s, tilt_s, tiles, steps) = refs
    cells = own_f.shape[0] // CELL
    count = first.shape[0]
    width = ROWS * CELL

    flip[0] = jnp.transpose(w_a[...].astype(F32)).astype(BF)
    flip[1] = jnp.transpose(w_b[...].astype(F32)).astype(BF)
    mix_f = mix[...].astype(F32)
    mix_t[...] = (jnp.transpose(mix_f) * 0.5).astype(BF)
    mix_o[...] = (mix_f * 0.25).astype(BF)
    scale_o[...] = jnp.transpose(jnp.broadcast_to(out_w[...] / CELL, (CELL, CELL)))
    high = out_w[...].astype(BF)
    low = (out_w[...] - high.astype(F32)).astype(BF)
    pad = jnp.zeros((6, CELL), F32)
    left = jnp.concatenate([radial[...].astype(F32), jnp.zeros((8, CELL), F32)], axis=0)
    right = jnp.concatenate([jnp.zeros((NB, CELL), F32), high.astype(F32), low.astype(F32), pad], axis=0)
    last[...] = jnp.concatenate([left, right], axis=1).astype(BF)
    radial_h = radial[...].astype(F32) * 0.5
    row_of = lax.broadcasted_iota(jnp.int32, (ROWS, width), 0)
    lane_of = lax.broadcasted_iota(jnp.int32, (ROWS, width), 1) // CELL
    onehot[...] = jnp.where(row_of == lane_of, 1.0, 0.0).astype(BF)
    centers = lax.broadcasted_iota(jnp.int32, (NB, CELL), 0).astype(F32) * (6.75 / NB)

    if stage == 0:
        total[...] = jnp.zeros_like(total)
    else:
        total[...] = remote[-1][...]
    if stage == 1:
        side[...] = jnp.zeros_like(side)

    picked, early = jnp.int32(0), jnp.int32(0)
    for t in range(count):
        block = second[t] // cells
        need = (jnp.minimum(live_a[t], live_b[t]) + UNIT - 1) // UNIT
        soon = (block == 0) & (early + need <= EARLY)
        early = early + jnp.where(soon, need, 0)
        take = (soon, (block < 2) & ~soon, block >= 2)[stage]
        tiles[picked] = jnp.int32(t)
        picked = picked + take.astype(jnp.int32)

    def prepare(s, so_far):
        t = tiles[s]
        cell = second[t] % cells
        pa[s] = tall(place_at(own_p, first[t]))
        if stage == 2:
            base = pl.multiple_of(t * PACKED, 16)
            fb[...] = remote[0][pl.ds(base, CELL), :]
            rest = remote[0][pl.ds(pl.multiple_of(base + CELL, 16), 16), :]
            pb[s] = rest.astype(F32)[0:8]
        else:
            def bring(feats, places):
                fb[...] = cell_at(feats, cell)
                pb[s] = tall(place_at(places, cell))

            if stage == 0:
                bring(own_f, own_p)
            else:
                pl.when(second[t] < cells)(functools.partial(bring, own_f, own_p))
                pl.when(second[t] >= cells)(functools.partial(bring, remote[0], remote[1]))
        num_a, num_b = live_a[t], live_b[t]
        swap = num_a > num_b
        feats_a, feats_b = cell_at(own_f, first[t]), fb[...]
        rows_f = jnp.where(swap, feats_b, feats_a)
        lanes_f = jnp.where(swap, feats_a, feats_b)
        rows_p, lanes_p = jnp.where(swap, pb[s], pa[s]), jnp.where(swap, pa[s], pb[s])
        w_r = jnp.where(swap, w_b[...], w_a[...])
        w_l = jnp.where(swap, flip[0], flip[1])
        proj_r[s] = dot(rows_f, w_r).astype(BF).astype(F32) * 0.5
        proj_l[s] = lax.dot_general(w_l, lanes_f, LAST, preferred_element_type=F32).astype(BF).astype(F32) * 0.5
        tall_p = jnp.transpose(rows_p)
        gaps = [tall_p[:, c : c + 1] - lanes_p[c : c + 1, :] for c in range(3)]
        dist[s] = gaps[0] * gaps[0] + gaps[1] * gaps[1] + gaps[2] * gaps[2]
        n = (jnp.minimum(num_a, num_b) + UNIT - 1) // UNIT
        steps[s] = n
        return so_far + n

    units = lax.fori_loop(0, picked, prepare, jnp.int32(0))

    proj_r[picked, 0:UNIT, :] = jnp.zeros((UNIT, CELL), F32)
    dist[picked, 0:UNIT, :] = jnp.zeros((UNIT, CELL), F32)

    def after(s, g):
        over = g + 1 >= steps[s]
        return jnp.where(over, s + 1, s), jnp.where(over, 0, g + 1)

    def rows_of(ref, where):
        return [ref[s, pl.ds(pl.multiple_of(g * UNIT, UNIT), UNIT), :] for s, g in where]

    def enter(where):
        r2 = jnp.concatenate(rows_of(dist, where), axis=0)
        weights = jnp.transpose(jnp.concatenate([radial_h, *rows_of(proj_r, where)], axis=0)).astype(BF)
        offset = jnp.concatenate(
            [jnp.broadcast_to(r2[k : k + 1, :], (NB, CELL)) - centers for k in range(ROWS)], axis=1
        )
        basis = jnp.exp(-2.0 * offset * offset)
        inputs = jnp.concatenate([basis.astype(BF), onehot[...]], axis=0)
        lanes = jnp.concatenate([proj_l[s] for s, g in where for _ in range(UNIT)], axis=1)
        return r2, dot(weights, inputs) + lanes, basis * offset

    def rest(where, r2, half, tilt):
        bend = jnp.tanh(half)
        up = 1 + bend
        latent = half * up
        slope = up + latent * (1 - bend)
        pre = dot(mix_t[...], latent.astype(BF))
        bend = jnp.tanh(pre)
        up = 1 + bend
        act = pre * up
        near = 1.0 - r2 / 8.0
        near = near * near
        envelope = jnp.concatenate([near[k : k + 1, :] for k in range(ROWS)], axis=1)
        d_pre = envelope * jnp.concatenate([scale_o[...]] * ROWS, axis=1) * (up + act * (1 - bend))
        d_latent = dot(mix_o[...], d_pre.astype(BF))
        d_summed = (d_latent * slope).astype(BF)
        both = dot(last[...], jnp.concatenate([d_summed, act.astype(BF)], axis=0))
        d_r2 = jnp.sum(both[:NB] * tilt, axis=0, keepdims=True)
        readout = both[NB : NB + 1] + both[NB + 1 : NB + 2]
        for k, (s, g) in enumerate(where):
            cut = [slice(j * CELL, (j + 1) * CELL) for j in range(k * UNIT, (k + 1) * UNIT)]
            at = pl.ds(pl.multiple_of(g * UNIT, UNIT), UNIT)
            slope_sum[s, at, :] = jnp.concatenate([d_r2[:, c] for c in cut], axis=0)
            read_sum[s, at, :] = jnp.concatenate([readout[:, c] for c in cut], axis=0)

    def spread(s, g):
        where = [(s, g)]
        while len(where) < UNITS:
            s, g = after(*where[-1])
            where.append((jnp.minimum(s, picked), jnp.where(s < picked, g, 0)))
        return where

    last_tile = jnp.maximum(picked - 1, 0)

    def begin(where):
        r2, half_v, tilt_v = enter(where)
        near_rows[...] = r2
        half_s[...] = half_v
        tilt_s[...] = tilt_v

    def edges(_, here):
        where = spread(*here)
        r2, half_v, tilt_v = near_rows[...], half_s[...], tilt_s[...]
        s, g = after(*where[-1])
        nxt = spread(jnp.minimum(s, picked), jnp.where(s < picked, g, 0))
        rest(where, r2, half_v, tilt_v)
        begin(nxt)
        return nxt[0]

    begin(spread(jnp.int32(0), jnp.int32(0)))
    lax.fori_loop(0, (units + UNITS - 1) // UNITS, edges, (jnp.int32(0), jnp.int32(0)))

    row_at = lax.broadcasted_iota(jnp.int32, (CELL, CELL), 0)
    lane_at = lax.broadcasted_iota(jnp.int32, (CELL, CELL), 1)

    def finish(s, _):
        t = tiles[s]
        num_a, num_b = live_a[t], live_b[t]
        swap = num_a > num_b
        rows_p, lanes_p = jnp.where(swap, pb[s], pa[s]), jnp.where(swap, pa[s], pb[s])
        live = (row_at < jnp.minimum(num_a, num_b)) & (lane_at < jnp.maximum(num_a, num_b))
        near = 1.0 - dist[s] / 8.0
        pull = 2.0 * (-4.0 * slope_sum[s] - near * (0.25 / CELL) * read_sum[s])
        pull = jnp.where(live, pull, 0.0)
        high = pull.astype(BF)
        low = (pull - high.astype(F32)).astype(BF)

        def with_ones(places):
            rows = jnp.concatenate([places[0:3], jnp.ones((1, CELL), F32), jnp.zeros((4, CELL), F32)], axis=0)
            rows = rows.astype(BF)
            return jnp.concatenate([rows, rows], axis=1)

        over_lanes = lax.dot_general(
            with_ones(lanes_p), jnp.concatenate([high, low], axis=1), LAST, preferred_element_type=F32
        )
        over_rows = dot(with_ones(rows_p), jnp.concatenate([high, low], axis=0))
        grad_r = rows_p * over_lanes[3:4] - over_lanes
        grad_l = lanes_p * over_rows[3:4] - over_rows
        grad_a = jnp.where(swap, grad_l, grad_r)
        grad_b = jnp.where(swap, grad_r, grad_l)
        here = pl.ds(pl.multiple_of(first[t] * CELL, CELL), CELL)
        total[:, here] = total[:, here] + grad_a[0:3]
        there = pl.ds(pl.multiple_of(second[t] % cells * CELL, CELL), CELL)

        def add(sums):
            sums[:, there] = sums[:, there] + grad_b[0:3]

        if stage == 0:
            add(total)
        elif stage == 1:
            pl.when(second[t] < cells)(functools.partial(add, total))
            pl.when(second[t] >= cells)(functools.partial(add, side))
        else:
            side[t] = grad_b
        return 0

    lax.fori_loop(0, picked, finish, 0)


def last_kernel(wanted, wanted_far, total, upper, corner, side, out):
    cells = total.shape[1] // CELL
    out[...] = -(total[...] + side[...])
    for slot in range(wanted.shape[0]):
        for asked, block, got in ((wanted, 2, upper), (wanted_far, 3, corner)):

            @pl.when(asked[slot] // cells == block)
            def _(asked=asked, got=got, slot=slot):
                here = pl.ds(pl.multiple_of(asked[slot] % cells * CELL, CELL), CELL)
                out[:, here] = out[:, here] - got[slot][0:3]


def called(kernel, prefetch, operands, out_shape, scratch=(), work=1.0, name=None, bring=False):
    if bring:
        scratch = [*scratch, *[pltpu.VMEM(x.shape, x.dtype) for x in operands]]
        scratch.append(pltpu.SemaphoreType.DMA((len(operands),)))
    return pl.pallas_call(
        kernel,
        grid_spec=pltpu.PrefetchScalarGridSpec(
            num_scalar_prefetch=len(prefetch),
            grid=(1,),
            in_specs=[pl.BlockSpec(memory_space=pltpu.HBM) if bring else VMEM] * len(operands),
            out_specs=jax.tree.map(lambda _: VMEM, out_shape),
            scratch_shapes=list(scratch),
        ),
        out_shape=out_shape,
        compiler_params=pltpu.CompilerParams(vmem_limit_bytes=(64000000 if bring else 40 << 20)),
        cost_estimate=pl.CostEstimate(flops=int(work * 1e9), bytes_accessed=1 << 20, transcendentals=0),
        name=name,
    )(*prefetch, *operands)


def on_device(
    positions,
    features,
    tile_first,
    tile_second,
    count_first,
    count_second,
    w_first,
    w_second,
    radial_weight,
    mix_weight,
    out_weight,
):
    slots = positions.shape[1]
    count = tile_first.shape[0]
    side_f = shifted(features, 0, 1)
    side_p = shifted(positions, 0, 1)
    asked = shifted(tile_second, -1, 0)
    asked_far = shifted(tile_second, -1, -1)

    scalars = (tile_first, tile_second, count_first, count_second)
    weights = (w_first, w_second, radial_weight, mix_weight, out_weight.reshape(1, -1))
    sums = jax.ShapeDtypeStruct((3, slots), F32)
    square = (count + 1, CELL, CELL)
    scratch = [
        pltpu.VMEM((2, CELL, CELL), BF),
        pltpu.VMEM((CELL, CELL), BF),
        pltpu.VMEM((CELL, CELL), BF),
        pltpu.VMEM((CELL, CELL), F32),
        pltpu.VMEM((24, 2 * CELL), BF),
        pltpu.VMEM((ROWS, ROWS * CELL), BF),
        *[pltpu.VMEM(square, F32)] * 5,
        pltpu.VMEM((CELL, CELL), BF),
        *[pltpu.VMEM((count, 8, CELL), F32)] * 2,
        pltpu.VMEM((ROWS, CELL), F32),
        pltpu.VMEM((CELL, ROWS * CELL), F32),
        pltpu.VMEM((NB, ROWS * CELL), F32),
        pltpu.SMEM((count + 1,), jnp.int32),
        pltpu.SMEM((count + 1,), jnp.int32),
    ]

    def tiles(stage, extra, outs, work):
        operands = (features, positions, *extra, *weights)
        return called(
            functools.partial(tile_kernel, stage), scalars, operands, outs, scratch, work,
            f"tiles{stage}", bring=stage == 0,
        )

    (total,) = tiles(0, (), (sums,), 8.0)
    packed = called(
        pack_kernel,
        (asked, asked_far),
        (features, positions, side_f, side_p),
        jax.ShapeDtypeStruct((count * PACKED, CELL), BF),
        name="pack",
    )
    upper_cells = shifted(packed, 1, 0)
    total, side = tiles(1, (side_f, side_p, total), (sums, sums), 8.0)
    grads = jax.ShapeDtypeStruct((count, 8, CELL), F32)
    total, grads = tiles(2, (upper_cells, total), (sums, grads), 16.0)
    from_upper = shifted(grads, -1, 0)
    from_corner = shifted(grads, -1, -1)
    side, _ = lax.optimization_barrier((side, grads))
    from_side = shifted(side, 0, -1)
    return called(
        last_kernel, (asked, asked_far), (total, from_upper, from_corner, from_side), sums, name="last"
    )


def solution(mesh):
    whole = ("grp", "dev")
    in_specs = (P(None, whole), P(whole, None), *[P(whole)] * 4, *[P()] * 5)
    return jax.shard_map(
        on_device, mesh=mesh, in_specs=in_specs, out_specs=P(None, whole), check_vma=False
    )
```

profile of v0, /device:TPU:0, one launch (start us, length us, event | category | flops | bytes accessed | tf_op | source)
XLA Modules:
  0.0 75.4 jit_solution(234511988108140592)
XLA Ops:
  0.0 0.5 collective-permute-start.2
  0.5 6.4 %collective-permute-start.1 = (s32[8]{0:T(128)}, s32[8]{0:T(128)S(1)}, u32[]{:S(2)}, u32[]{:S(2)}) collective-permute-start(s32[8]{0:T(128)} %second.5), channel_id=1, source_target_pairs={{0,31},{1,24},{2,25},{3,26},{4,27},{5,28},{6,29},{7,30},{8,7},{9,0... | collective-permute-start | bytes 104 | tf_op jit(solution)/shard_map/ppermute | solution.py:33
  6.9 0.5 collective-permute-start
  7.4 0.0 collective-permute-start.3
  7.4 0.0 copy-start
  7.4 0.0 copy-start.1
  7.4 7.0 %tiles0.1.refs_2_ = f32[3,4096]{1,0:T(4,128)} custom-call(s32[8]{0:T(128)} %first.5, s32[8]{0:T(128)} %second.5, s32[8]{0:T(128)} %live_a.5, s32[8]{0:T(128)} %live_b.5, bf16[4096,128]{1,0:T(8,128)(2,1)} %own_f.7, bf16[3,4096]{1,0:T(4,128)(2,1)} %own_p.7, bf16[128,128]{1,0:T(8,128)(2,1)} %refs_2_.3, bf16[128,128]{1,0:T(8,128)(2,1)} %refs_3_.5, ...), custom_call_target="tpu_custom_call" | custom-call | flops 8000000000 | bytes 1048576 | tf_op jit(solution)/shard_map/tiles0/pallas_call | solution.py:299
  14.4 0.0 copy-start.2
  14.4 0.0 copy-start.3
  14.5 0.0 copy-start.4
  14.5 0.0 copy-start.5
  14.5 0.0 copy-start.6
  14.5 0.0 copy-start.7
  14.5 0.0 copy-start.8
  14.5 0.0 copy-start.9
  14.5 0.0 copy-start.10
  14.5 0.0 copy-start.11
  14.6 0.0 collective-permute-done.1._.wanted_far
  14.6 0.0 collective-permute-done.wanted
  14.6 3.0 %collective-permute-done.3.side_p.refs_1_ = bf16[3,4096]{1,0:T(4,128)(2,1)S(1)} collective-permute-done((bf16[3,4096]{1,0:T(4,128)(2,1)}, bf16[3,4096]{1,0:T(4,128)(2,1)S(1)}, u32[]{:S(2)}, u32[]{:S(2)}) %collective-permute-start.3) | collective-permute-done | bytes 24608 | tf_op jit(solution)/shard_map/ppermute | solution.py:25
  17.6 0.0 collective-permute-done.2.side_f.refs_0_
  17.6 0.0 copy-done
  17.6 0.0 copy-done.1
  17.6 0.7 pack.1
  18.3 2.0 %collective-permute-start.4 = (bf16[1152,128]{1,0:T(8,128)(2,1)S(1)}, bf16[1152,128]{1,0:T(8,128)(2,1)S(1)}, u32[]{:S(2)}, u32[]{:S(2)}) collective-permute-start(bf16[1152,128]{1,0:T(8,128)(2,1)S(1)} %pack.1), channel_id=1, source_target_pairs={{0,8},{8,16},{16,24},{24,0},{1,9},{9,17},{17,25},{25,1},{2,10},{10... | collective-permute-start | bytes 884744 | tf_op jit(solution)/shard_map/ppermute | solution.py:27
  20.3 0.0 copy-done.2
  20.3 0.0 copy-done.3
  20.3 0.0 copy-done.4
  20.3 0.0 copy-done.5
  20.3 0.0 copy-done.6
  20.4 0.0 copy-done.7
  20.4 0.0 copy-done.8
  20.4 0.0 copy-done.9
  20.4 0.0 copy-done.10
  20.4 0.0 copy-done.11
  20.4 27.6 %tiles1.1 = (f32[3,4096]{1,0:T(4,128)S(1)}, f32[3,4096]{1,0:T(4,128)S(1)}) custom-call(s32[8]{0:T(128)S(1)} %copy-done.7, s32[8]{0:T(128)S(1)} %copy-done.6, s32[8]{0:T(128)S(1)} %copy-done.8, s32[8]{0:T(128)S(1)} %copy-done.9, bf16[4096,128]{1,0:T(8,128)(2,1)S(1)} %copy-done, bf16[3,4096]{1,0:T(4,128)(2,1)S(1)} %copy-done.1, ...), custom_call_target="tpu_custom_call" | custom-call | flops 8000000000 | bytes 1048576 | tf_op jit(solution)/shard_map/tiles1/pallas_call | solution.py:299
  48.0 0.0 collective-permute-done.4.refs_0_
  48.1 14.0 %tiles2.1 = (f32[3,4096]{1,0:T(4,128)S(1)}, f32[8,8,128]{2,1,0:T(8,128)S(1)}) custom-call(s32[8]{0:T(128)S(1)} %copy-done.7, s32[8]{0:T(128)S(1)} %copy-done.6, s32[8]{0:T(128)S(1)} %copy-done.8, s32[8]{0:T(128)S(1)} %copy-done.9, bf16[4096,128]{1,0:T(8,128)(2,1)S(1)} %copy-done, bf16[3,4096]{1,0:T(4,128)(2,1)S(1)} %copy-done.1, ...), custom_call_target="tpu_custom_call" | custom-call | flops 16000000000 | bytes 1048576 | tf_op jit(solution)/shard_map/tiles2/pallas_call | solution.py:299
  62.1 7.9 %collective-permute-start.7 = (f32[3,4096]{1,0:T(4,128)S(1)}, f32[3,4096]{1,0:T(4,128)S(1)}, u32[]{:S(2)}, u32[]{:S(2)}) collective-permute-start(f32[3,4096]{1,0:T(4,128)S(1)} %get-tuple-element.14), channel_id=1, source_target_pairs={{0,7},{1,0},{2,1},{3,2},{4,3},{5,4},{6,5},{7,6},{8,15},{9,8},{10,9... | collective-permute-start | bytes 147464 | tf_op jit(solution)/shard_map/ppermute | solution.py:25
  69.9 0.0 collective-permute-start.6
  69.9 0.0 collective-permute-start.5
  69.9 3.3 %collective-permute-done.6.corner = f32[8,8,128]{2,1,0:T(8,128)S(1)} collective-permute-done((f32[8,8,128]{2,1,0:T(8,128)S(1)}, f32[8,8,128]{2,1,0:T(8,128)S(1)}, u32[]{:S(2)}, u32[]{:S(2)}) %collective-permute-start.6) | collective-permute-done | bytes 32800 | tf_op jit(solution)/shard_map/ppermute | solution.py:33
  73.3 0.7 collective-permute-done.5.upper
  74.0 0.0 collective-permute-done.7.side
  74.0 1.4 %last.1 = f32[3,4096]{1,0:T(4,128)} custom-call(s32[8]{0:T(128)S(1)} %collective-permute-done.wanted, s32[8]{0:T(128)S(1)} %collective-permute-done.1._.wanted_far, f32[3,4096]{1,0:T(4,128)S(1)} %get-tuple-element.11.total, f32[8,8,128]{2,1,0:T(8,128)S(1)} %collective-permute-done.5.upper, f32[8,8,128]{2,1,0:T(8,128)S(1)} %collective-permute-done.6.corner, ...), custom_call_target="tpu_custom_call" | custom-call | flops 1000000000 | bytes 1048576 | tf_op jit(solution)/shard_map/last/pallas_call | solution.py:299
Async XLA Ops:
  0.0 17.6 %collective-permute-start.2 = (bf16[4096,128]{1,0:T(8,128)(2,1)}, bf16[4096,128]{1,0:T(8,128)(2,1)S(1)}, u32[]{:S(2)}, u32[]{:S(2)}) collective-permute-start(bf16[4096,128]{1,0:T(8,128)(2,1)} %own_f.7), channel_id=1, source_target_pairs={{0,1},{1,2},{2,3},{3,4},{4,5},{5,6},{6,7},{7,0},{8,9},{9,10},{10,1... | collective-permute-start | bytes 3145736 | tf_op jit(solution)/shard_map/ppermute | solution.py:25
  0.5 14.1 %collective-permute-start.1 = (s32[8]{0:T(128)}, s32[8]{0:T(128)S(1)}, u32[]{:S(2)}, u32[]{:S(2)}) collective-permute-start(s32[8]{0:T(128)} %second.5), channel_id=1, source_target_pairs={{0,31},{1,24},{2,25},{3,26},{4,27},{5,28},{6,29},{7,30},{8,7},{9,0... | collective-permute-start | bytes 104 | tf_op jit(solution)/shard_map/ppermute | solution.py:33
  6.9 7.7 %collective-permute-start = (s32[8]{0:T(128)}, s32[8]{0:T(128)S(1)}, u32[]{:S(2)}, u32[]{:S(2)}) collective-permute-start(s32[8]{0:T(128)} %second.5), channel_id=1, source_target_pairs={{0,24},{8,0},{16,8},{24,16},{1,25},{9,1},{17,9},{25,17},{2,26},{10... | collective-permute-start | bytes 104 | tf_op jit(solution)/shard_map/ppermute | solution.py:27
  7.4 10.1 %collective-permute-start.3 = (bf16[3,4096]{1,0:T(4,128)(2,1)}, bf16[3,4096]{1,0:T(4,128)(2,1)S(1)}, u32[]{:S(2)}, u32[]{:S(2)}) collective-permute-start(bf16[3,4096]{1,0:T(4,128)(2,1)} %own_p.7), channel_id=1, source_target_pairs={{0,1},{1,2},{2,3},{3,4},{4,5},{5,6},{6,7},{7,0},{8,9},{9,10},{10,1... | collective-permute-start | bytes 73736 | tf_op jit(solution)/shard_map/ppermute | solution.py:25
  7.4 10.1 %copy-start = (bf16[4096,128]{1,0:T(8,128)(2,1)S(1)}, bf16[4096,128]{1,0:T(8,128)(2,1)}, u32[]{:S(2)}) copy-start(bf16[4096,128]{1,0:T(8,128)(2,1)} %own_f.7) | copy-start | bytes 3145732
  7.4 10.1 %copy-start.1 = (bf16[3,4096]{1,0:T(4,128)(2,1)S(1)}, bf16[3,4096]{1,0:T(4,128)(2,1)}, u32[]{:S(2)}) copy-start(bf16[3,4096]{1,0:T(4,128)(2,1)} %own_p.7) | copy-start | bytes 73732
  14.4 5.9 %copy-start.2 = (bf16[128,128]{1,0:T(8,128)(2,1)S(1)}, bf16[128,128]{1,0:T(8,128)(2,1)}, u32[]{:S(2)}) copy-start(bf16[128,128]{1,0:T(8,128)(2,1)} %refs_2_.3) | copy-start | bytes 98308
  14.4 5.9 %copy-start.3 = (bf16[128,128]{1,0:T(8,128)(2,1)S(1)}, bf16[128,128]{1,0:T(8,128)(2,1)}, u32[]{:S(2)}) copy-start(bf16[128,128]{1,0:T(8,128)(2,1)} %refs_3_.5) | copy-start | bytes 98308
  14.5 5.9 %copy-start.4 = (bf16[128,128]{1,0:T(8,128)(2,1)S(1)}, bf16[128,128]{1,0:T(8,128)(2,1)}, u32[]{:S(2)}) copy-start(bf16[128,128]{1,0:T(8,128)(2,1)} %refs_5_.3) | copy-start | bytes 98308
  14.5 5.9 %copy-start.5 = (bf16[16,128]{1,0:T(8,128)(2,1)S(1)}, bf16[16,128]{1,0:T(8,128)(2,1)}, u32[]{:S(2)}) copy-start(bf16[16,128]{1,0:T(8,128)(2,1)} %refs_4_.3) | copy-start | bytes 12292
  14.5 5.9 %copy-start.6 = (s32[8]{0:T(128)S(1)}, s32[8]{0:T(128)}, u32[]{:S(2)}) copy-start(s32[8]{0:T(128)} %second.5) | copy-start | bytes 100
  14.5 5.9 %copy-start.7 = (s32[8]{0:T(128)S(1)}, s32[8]{0:T(128)}, u32[]{:S(2)}) copy-start(s32[8]{0:T(128)} %first.5) | copy-start | bytes 100
  14.5 5.9 %copy-start.8 = (s32[8]{0:T(128)S(1)}, s32[8]{0:T(128)}, u32[]{:S(2)}) copy-start(s32[8]{0:T(128)} %live_a.5) | copy-start | bytes 100
  14.5 5.9 %copy-start.9 = (s32[8]{0:T(128)S(1)}, s32[8]{0:T(128)}, u32[]{:S(2)}) copy-start(s32[8]{0:T(128)} %live_b.5) | copy-start | bytes 100
  14.5 5.9 %copy-start.10 = (f32[128]{0:T(128)S(1)}, f32[128]{0:T(128)}, u32[]{:S(2)}) copy-start(f32[128]{0:T(128)} %param.21) | copy-start | bytes 1540
  14.5 5.9 %copy-start.11 = (f32[3,4096]{1,0:T(4,128)S(1)}, f32[3,4096]{1,0:T(4,128)}, u32[]{:S(2)}) copy-start(f32[3,4096]{1,0:T(4,128)} %tiles0.1.refs_2_) | copy-start | bytes 147460
  18.3 29.8 %collective-permute-start.4 = (bf16[1152,128]{1,0:T(8,128)(2,1)S(1)}, bf16[1152,128]{1,0:T(8,128)(2,1)S(1)}, u32[]{:S(2)}, u32[]{:S(2)}) collective-permute-start(bf16[1152,128]{1,0:T(8,128)(2,1)S(1)} %pack.1), channel_id=1, source_target_pairs={{0,8},{8,16},{16,24},{24,0},{1,9},{9,17},{17,25},{25,1},{2,10},{10... | collective-permute-start | bytes 884744 | tf_op jit(solution)/shard_map/ppermute | solution.py:27
  62.1 11.9 %collective-permute-start.7 = (f32[3,4096]{1,0:T(4,128)S(1)}, f32[3,4096]{1,0:T(4,128)S(1)}, u32[]{:S(2)}, u32[]{:S(2)}) collective-permute-start(f32[3,4096]{1,0:T(4,128)S(1)} %get-tuple-element.14), channel_id=1, source_target_pairs={{0,7},{1,0},{2,1},{3,2},{4,3},{5,4},{6,5},{7,6},{8,15},{9,8},{10,9... | collective-permute-start | bytes 147464 | tf_op jit(solution)/shard_map/ppermute | solution.py:25
  69.9 3.3 %collective-permute-start.6 = (f32[8,8,128]{2,1,0:T(8,128)S(1)}, f32[8,8,128]{2,1,0:T(8,128)S(1)}, u32[]{:S(2)}, u32[]{:S(2)}) collective-permute-start(f32[8,8,128]{2,1,0:T(8,128)S(1)} %get-tuple-element.12), channel_id=1, source_target_pairs={{0,31},{1,24},{2,25},{3,26},{4,27},{5,28},{6,29},{7,30},{8,7},{9,0... | collective-permute-start | bytes 98312 | tf_op jit(solution)/shard_map/ppermute | solution.py:33
  69.9 4.0 %collective-permute-start.5 = (f32[8,8,128]{2,1,0:T(8,128)S(1)}, f32[8,8,128]{2,1,0:T(8,128)S(1)}, u32[]{:S(2)}, u32[]{:S(2)}) collective-permute-start(f32[8,8,128]{2,1,0:T(8,128)S(1)} %get-tuple-element.12), channel_id=1, source_target_pairs={{0,24},{8,0},{16,8},{24,16},{1,25},{9,1},{17,9},{25,17},{2,26},{10... | collective-permute-start | bytes 98312 | tf_op jit(solution)/shard_map/ppermute | solution.py:27
where the time goes:
time: 75.1 us; the launch traced here: 75.4 us
  Pallas kernels  50.8 us (68%)
  starting transfers between devices  17.3 us (23%)
  waiting for transfers between devices  7.04 us (9%)
    pallas_call x5, Pallas kernels, called(): pl.pallas_call(kernel, grid_spec=pltpu.PrefetchScalarGridSpec(num_scalar_...  50.8 us
    ppermute x3, starting transfers between devices, shifted(): lax.ppermute(array, 'dev', [(i, (i + members) % n_dev) for i in range(n_d...  8.35 us
    ppermute x2, starting transfers between devices, shifted(): return lax.ppermute(array, ('grp', 'dev'), pairs)  6.41 us
    ppermute x2, waiting for transfers between devices, shifted(): return lax.ppermute(array, ('grp', 'dev'), pairs)  3.34 us
    ppermute x3, waiting for transfers between devices, shifted(): lax.ppermute(array, 'dev', [(i, (i + members) % n_dev) for i in range(n_d...  2.99 us
    ppermute x3, starting transfers between devices, shifted(): lax.ppermute(array, 'grp', [(i, (i + groups) % n_grp) for i in range(n_gr...  2.57 us
  transfers between devices with their start and end apart: 8, of which 3 were waited for; matrix products, arithmetic and copies ran while one was open for 0% of the time, Pallas kernels for 46%

commit v1 on v0

--- a/solution.py
+++ b/solution.py
@@ -62,6 +62,44 @@
 
         pl.when(block == 2)(functools.partial(put, own_f, own_p))
         pl.when(block == 3)(functools.partial(put, side_f, side_p))
+
+
+def units_of(rows, lanes):
+    thirds = rows // 32 * 3 + jnp.minimum(3, (rows % 32 + 7) // 8)
+    return jnp.where(lanes > 96, (rows + 7) // 8, jnp.where(lanes > 64, thirds, (rows + 15) // 16))
+
+
+def kind_of(lanes):
+    return jnp.where(lanes > 96, 0, jnp.where(lanes > 64, 1, 2))
+
+
+def folded(kind, rows, lane_at):
+    eight = [rows[k : k + 8] for k in range(0, CELL, 8)]
+    out = []
+    if kind == 1:
+        for q in range(0, 16, 4):
+            for u in range(3):
+                moved = pltpu.roll(eight[q + 3], 96 - 32 * u, 1)
+                out.append(jnp.where(lane_at[:8] < 96, eight[q + u], moved))
+    else:
+        for q in range(0, 8, 2):
+            out.append(jnp.where(lane_at[:8] < 64, eight[q], pltpu.roll(eight[q + 1], 64, 1)))
+    return jnp.concatenate(out, axis=0)
+
+
+def unfolded(kind, rows, lane_at):
+    eight = [rows[k : k + 8] for k in range(0, CELL, 8)]
+    out = []
+    if kind == 1:
+        for q in range(0, 12, 3):
+            out.extend(eight[q : q + 3])
+            first, second, third = (pltpu.roll(eight[q + u], 32 * u + 32, 1) for u in range(3))
+            out.append(jnp.where(lane_at[:8] < 32, first, jnp.where(lane_at[:8] < 64, second, third)))
+    else:
+        for q in range(4):
+            out.extend((eight[q], pltpu.roll(eight[q], 64, 1)))
+        out.extend(eight[8:])
+    return jnp.concatenate(out, axis=0)
 
 
 def tile_kernel(
@@ -83,10 +121,9 @@
             copy.wait()
         refs = refs[:-8]
     (
-     flip, mix_t, mix_o, scale_o, last, onehot, proj_r, proj_l, dist, slope_sum, read_sum, fb, pa, pb, near_rows, half_s, tilt_s, tiles, steps) = refs
+     flip, mix_t, mix_o, scale_o, last, onehot, proj_r, plain, dist, slope_sum, read_sum, proj_l, fb, pa, pb, near_rows, half_s, tilt_s, tiles, steps, kinds) = refs
     cells = own_f.shape[0] // CELL
     count = first.shape[0]
-    width = ROWS * CELL
 
     flip[0] = jnp.transpose(w_a[...].astype(F32)).astype(BF)
     flip[1] = jnp.transpose(w_b[...].astype(F32)).astype(BF)
@@ -101,9 +138,13 @@
     right = jnp.concatenate([jnp.zeros((NB, CELL), F32), high.astype(F32), low.astype(F32), pad], axis=0)
     last[...] = jnp.concatenate([left, right], axis=1).astype(BF)
     radial_h = radial[...].astype(F32) * 0.5
-    row_of = lax.broadcasted_iota(jnp.int32, (ROWS, width), 0)
-    lane_of = lax.broadcasted_iota(jnp.int32, (ROWS, width), 1) // CELL
-    onehot[...] = jnp.where(row_of == lane_of, 1.0, 0.0).astype(BF)
+    row_of = lax.broadcasted_iota(jnp.int32, (2 * UNIT, UNIT * CELL), 0)
+    at_lane = lax.broadcasted_iota(jnp.int32, (2 * UNIT, UNIT * CELL), 1)
+    for kind, bound in enumerate((128, 96, 64)):
+        held_row = at_lane // CELL + jnp.where(at_lane % CELL < bound, 0, UNIT)
+        onehot[kind] = jnp.where(row_of == held_row, 1.0, 0.0).astype(BF)
+    row_at = lax.broadcasted_iota(jnp.int32, (CELL, CELL), 0)
+    lane_at = lax.broadcasted_iota(jnp.int32, (CELL, CELL), 1)
     centers = lax.broadcasted_iota(jnp.int32, (NB, CELL), 0).astype(F32) * (6.75 / NB)
 
     if stage == 0:
@@ -116,7 +157,7 @@
     picked, early = jnp.int32(0), jnp.int32(0)
     for t in range(count):
         block = second[t] // cells
-        need = (jnp.minimum(live_a[t], live_b[t]) + UNIT - 1) // UNIT
+        need = units_of(jnp.minimum(live_a[t], live_b[t]), jnp.maximum(live_a[t], live_b[t]))
         soon = (block == 0) & (early + need <= EARLY)
         early = early + jnp.where(soon, need, 0)
         take = (soon, (block < 2) & ~soon, block >= 2)[stage]
@@ -151,11 +192,32 @@
         w_r = jnp.where(swap, w_b[...], w_a[...])
         w_l = jnp.where(swap, flip[0], flip[1])
         proj_r[s] = dot(rows_f, w_r).astype(BF).astype(F32) * 0.5
-        proj_l[s] = lax.dot_general(w_l, lanes_f, LAST, preferred_element_type=F32).astype(BF).astype(F32) * 0.5
+        lane_proj = lax.dot_general(w_l, lanes_f, LAST, preferred_element_type=F32).astype(BF).astype(F32) * 0.5
         tall_p = jnp.transpose(rows_p)
         gaps = [tall_p[:, c : c + 1] - lanes_p[c : c + 1, :] for c in range(3)]
-        dist[s] = gaps[0] * gaps[0] + gaps[1] * gaps[1] + gaps[2] * gaps[2]
-        n = (jnp.minimum(num_a, num_b) + UNIT - 1) // UNIT
+        r2 = gaps[0] * gaps[0] + gaps[1] * gaps[1] + gaps[2] * gaps[2]
+        plain[s] = r2
+        lanes = jnp.maximum(num_a, num_b)
+        kind = kind_of(lanes)
+
+        @pl.when(kind == 0)
+        def _():
+            dist[s] = r2
+            proj_l[s, 0] = lane_proj
+
+        @pl.when(kind == 1)
+        def _():
+            dist[s, 0:96, :] = folded(1, r2, lane_at)
+            for u in range(3):
+                proj_l[s, u] = jnp.where(lane_at < 96, lane_proj, pltpu.roll(lane_proj, 96 - 32 * u, 1))
+
+        @pl.when(kind == 2)
+        def _():
+            dist[s, 0:32, :] = folded(2, r2, lane_at)
+            proj_l[s, 0] = jnp.where(lane_at < 64, lane_proj, pltpu.roll(lane_proj, 64, 1))
+
+        kinds[s] = kind
+        n = units_of(jnp.minimum(num_a, num_b), lanes)
         steps[s] = n
         return so_far + n
 
@@ -163,6 +225,7 @@
 
     proj_r[picked, 0:UNIT, :] = jnp.zeros((UNIT, CELL), F32)
     dist[picked, 0:UNIT, :] = jnp.zeros((UNIT, CELL), F32)
+    kinds[picked] = jnp.int32(0)
 
     def after(s, g):
         over = g + 1 >= steps[s]
@@ -173,14 +236,24 @@
 
     def enter(where):
         r2 = jnp.concatenate(rows_of(dist, where), axis=0)
-        weights = jnp.transpose(jnp.concatenate([radial_h, *rows_of(proj_r, where)], axis=0)).astype(BF)
+        firsts, ones, lanes = [], [], []
+        for k, (s, g) in enumerate(where):
+            kind = kinds[s]
+            third, part = g // 3, g % 3
+            main = jnp.where(kind == 0, UNIT * g, jnp.where(kind == 1, 32 * third + UNIT * part, 2 * UNIT * g))
+            more = jnp.where(kind == 0, UNIT * g, jnp.where(kind == 1, 32 * third + 3 * UNIT, 2 * UNIT * g + UNIT))
+            for base in (main, more):
+                firsts.append(proj_r[s, pl.ds(pl.multiple_of(base, UNIT), UNIT), :])
+            blank = jnp.zeros((2 * UNIT, UNIT * CELL), BF)
+            ones.append(jnp.concatenate([onehot[kind] if j == k else blank for j in range(UNITS)], axis=1))
+            lanes.extend([proj_l[s, jnp.where(kind == 1, part, 0)]] * UNIT)
+        weights = jnp.transpose(jnp.concatenate([radial_h, *firsts], axis=0)).astype(BF)
         offset = jnp.concatenate(
             [jnp.broadcast_to(r2[k : k + 1, :], (NB, CELL)) - centers for k in range(ROWS)], axis=1
         )
         basis = jnp.exp(-2.0 * offset * offset)
-        inputs = jnp.concatenate([basis.astype(BF), onehot[...]], axis=0)
-        lanes = jnp.concatenate([proj_l[s] for s, g in where for _ in range(UNIT)], axis=1)
-        return r2, dot(weights, inputs) + lanes, basis * offset
+        inputs = jnp.concatenate([basis.astype(BF), *ones], axis=0)
+        return r2, dot(weights, inputs) + jnp.concatenate(lanes, axis=1), basis * offset
 
     def rest(where, r2, half, tilt):
         bend = jnp.tanh(half)
@@ -233,16 +306,20 @@
     begin(spread(jnp.int32(0), jnp.int32(0)))
     lax.fori_loop(0, (units + UNITS - 1) // UNITS, edges, (jnp.int32(0), jnp.int32(0)))
 
-    row_at = lax.broadcasted_iota(jnp.int32, (CELL, CELL), 0)
-    lane_at = lax.broadcasted_iota(jnp.int32, (CELL, CELL), 1)
-
     def finish(s, _):
         t = tiles[s]
         num_a, num_b = live_a[t], live_b[t]
         swap = num_a > num_b
         rows_p, lanes_p = jnp.where(swap, pb[s], pa[s]), jnp.where(swap, pa[s], pb[s])
         live = (row_at < jnp.minimum(num_a, num_b)) & (lane_at < jnp.maximum(num_a, num_b))
-        near = 1.0 - dist[s] / 8.0
+        for kind in (1, 2):
+
+            @pl.when(kinds[s] == kind)
+            def _(kind=kind):
+                slope_sum[s] = unfolded(kind, slope_sum[s], lane_at)
+                read_sum[s] = unfolded(kind, read_sum[s], lane_at)
+
+        near = 1.0 - plain[s] / 8.0
         pull = 2.0 * (-4.0 * slope_sum[s] - near * (0.25 / CELL) * read_sum[s])
         pull = jnp.where(live, pull, 0.0)
         high = pull.astype(BF)
@@ -342,15 +419,15 @@
         pltpu.VMEM((CELL, CELL), BF),
         pltpu.VMEM((CELL, CELL), F32),
         pltpu.VMEM((24, 2 * CELL), BF),
-        pltpu.VMEM((ROWS, ROWS * CELL), BF),
+        pltpu.VMEM((3, 2 * UNIT, UNIT * CELL), BF),
         *[pltpu.VMEM(square, F32)] * 5,
+        pltpu.VMEM((count + 1, 3, CELL, CELL), F32),
         pltpu.VMEM((CELL, CELL), BF),
         *[pltpu.VMEM((count, 8, CELL), F32)] * 2,
         pltpu.VMEM((ROWS, CELL), F32),
         pltpu.VMEM((CELL, ROWS * CELL), F32),
         pltpu.VMEM((NB, ROWS * CELL), F32),
-        pltpu.SMEM((count + 1,), jnp.int32),
-        pltpu.SMEM((count + 1,), jnp.int32),
+        *[pltpu.SMEM((count + 1,), jnp.int32)] * 3,
     ]
 
     def tiles(stage, extra, outs, work):

time: 75.1 us -> 70.9 us (0.944)
  Pallas kernels: 50.8 us -> 40.9 us
  starting transfers between devices: 17.3 us -> 26.8 us
  waiting for transfers between devices: 7.04 us -> 2.68 us
    pallas_call x5, Pallas kernels: 50.8 us -> 40.9 us  [called(): pl.pallas_call(kernel, grid_spec=pltpu.PrefetchScalarGridSpec(num_scalar_...]
    ppermute x3, starting transfers between devices: 8.35 us -> 15.5 us  [shifted(): lax.ppermute(array, 'dev', [(i, (i + members) % n_dev) for i in range(n_d...]
    ppermute x3, waiting for transfers between devices: 2.99 us -> 0.01 us  [shifted(): lax.ppermute(array, 'dev', [(i, (i + members) % n_dev) for i in range(n_d...]
    ppermute x3, starting transfers between devices: 2.57 us -> 4.92 us  [shifted(): lax.ppermute(array, 'grp', [(i, (i + groups) % n_grp) for i in range(n_gr...]
    ppermute x2, waiting for transfers between devices: 3.34 us -> 2.07 us  [shifted(): return lax.ppermute(array, ('grp', 'dev'), pairs)]
  transfers between devices with their start and end apart: 8 -> 8, of which waited for: 3 -> 2; matrix products, arithmetic and copies ran while one was open for 0% -> 0% of each run, Pallas kernels for 46% -> 30%
where the time goes in v1:
time: 70.9 us; the launch traced here: 70.6 us
  Pallas kernels  40.9 us (58%)
  starting transfers between devices  26.8 us (38%)
  waiting for transfers between devices  2.68 us (4%)
    pallas_call x5, Pallas kernels, called(): pl.pallas_call(kernel, grid_spec=pltpu.PrefetchScalarGridSpec(num_scalar_...  40.9 us
    ppermute x3, starting transfers between devices, shifted(): lax.ppermute(array, 'dev', [(i, (i + members) % n_dev) for i in range(n_d...  15.5 us
    ppermute x2, starting transfers between devices, shifted(): return lax.ppermute(array, ('grp', 'dev'), pairs)  6.41 us
    ppermute x3, starting transfers between devices, shifted(): lax.ppermute(array, 'grp', [(i, (i + groups) % n_grp) for i in range(n_gr...  4.92 us
    ppermute x2, waiting for transfers between devices, shifted(): return lax.ppermute(array, ('grp', 'dev'), pairs)  2.07 us
  transfers between devices with their start and end apart: 8, of which 2 were waited for; matrix products, arithmetic and copies ran while one was open for 0% of the time, Pallas kernels for 30%

profile of v1, /device:TPU:0, one launch (start us, length us, event | category | flops | bytes accessed | tf_op | source)
XLA Modules:
  0.0 70.6 jit_solution(2825645355446488730)
XLA Ops:
  0.0 0.5 collective-permute-start.2
  0.5 6.4 %collective-permute-start.1 = (s32[8]{0:T(128)}, s32[8]{0:T(128)S(1)}, u32[]{:S(2)}, u32[]{:S(2)}) collective-permute-start(s32[8]{0:T(128)} %second.5), channel_id=1, source_target_pairs={{0,31},{1,24},{2,25},{3,26},{4,27},{5,28},{6,29},{7,30},{8,7},{9,0... | collective-permute-start | bytes 104 | tf_op jit(solution)/shard_map/ppermute | solution.py:33
  6.9 0.5 collective-permute-start
  7.4 0.0 collective-permute-start.3
  7.4 0.0 copy-start
  7.4 0.0 copy-start.1
  7.4 10.2 %tiles0.1.refs_2_ = f32[3,4096]{1,0:T(4,128)} custom-call(s32[8]{0:T(128)} %first.5, s32[8]{0:T(128)} %second.5, s32[8]{0:T(128)} %live_a.5, s32[8]{0:T(128)} %live_b.5, bf16[4096,128]{1,0:T(8,128)(2,1)} %own_f.7, bf16[3,4096]{1,0:T(4,128)(2,1)} %own_p.7, bf16[128,128]{1,0:T(8,128)(2,1)} %refs_2_.3, bf16[128,128]{1,0:T(8,128)(2,1)} %refs_3_.5, ...), custom_call_target="tpu_custom_call" | custom-call | flops 8000000000 | bytes 1048576 | tf_op jit(solution)/shard_map/tiles0/pallas_call | solution.py:376
  17.6 0.0 copy-start.2
  17.7 0.0 copy-start.3
  17.7 0.0 copy-start.4
  17.7 0.0 copy-start.5
  17.7 0.0 copy-start.6
  17.7 0.0 copy-start.7
  17.7 0.0 copy-start.8
  17.7 0.0 copy-start.9
  17.7 0.0 copy-start.10
  17.7 0.0 copy-start.11
  17.8 0.0 collective-permute-done.1._.wanted_far
  17.8 0.0 collective-permute-done.wanted
  17.8 0.0 collective-permute-done.3.side_p.refs_1_
  17.8 0.0 collective-permute-done.2.side_f.refs_0_
  17.8 0.0 copy-done
  17.8 0.0 copy-done.1
  17.8 0.7 %pack.1 = bf16[1152,128]{1,0:T(8,128)(2,1)S(1)} custom-call(s32[8]{0:T(128)S(1)} %collective-permute-done.wanted, s32[8]{0:T(128)S(1)} %collective-permute-done.1._.wanted_far, bf16[4096,128]{1,0:T(8,128)(2,1)S(1)} %copy-done, bf16[3,4096]{1,0:T(4,128)(2,1)S(1)} %copy-done.1, bf16[4096,128]{1,0:T(8,128)(2,1)S(1)} %collective-permute-done.2.side_f.refs_0_, ...), custom_call_target="tpu_custom_call" | custom-call | flops 1000000000 | bytes 1048576 | tf_op jit(solution)/shard_map/pack/pallas_call | solution.py:376
  18.5 1.8 %collective-permute-start.4 = (bf16[1152,128]{1,0:T(8,128)(2,1)S(1)}, bf16[1152,128]{1,0:T(8,128)(2,1)S(1)}, u32[]{:S(2)}, u32[]{:S(2)}) collective-permute-start(bf16[1152,128]{1,0:T(8,128)(2,1)S(1)} %pack.1), channel_id=1, source_target_pairs={{0,8},{8,16},{16,24},{24,0},{1,9},{9,17},{17,25},{25,1},{2,10},{10... | collective-permute-start | bytes 884744 | tf_op jit(solution)/shard_map/ppermute | solution.py:27
  20.3 0.0 copy-done.2
  20.3 0.0 copy-done.3
  20.3 0.0 copy-done.4
  20.3 0.0 copy-done.5
  20.4 0.0 copy-done.6
  20.4 0.0 copy-done.7
  20.4 0.0 copy-done.8
  20.4 0.0 copy-done.9
  20.4 0.0 copy-done.10
  20.4 0.0 copy-done.11
  20.4 11.3 %tiles1.1 = (f32[3,4096]{1,0:T(4,128)S(1)}, f32[3,4096]{1,0:T(4,128)S(1)}) custom-call(s32[8]{0:T(128)S(1)} %copy-done.7, s32[8]{0:T(128)S(1)} %copy-done.6, s32[8]{0:T(128)S(1)} %copy-done.8, s32[8]{0:T(128)S(1)} %copy-done.9, bf16[4096,128]{1,0:T(8,128)(2,1)S(1)} %copy-done, bf16[3,4096]{1,0:T(4,128)(2,1)S(1)} %copy-done.1, ...), custom_call_target="tpu_custom_call" | custom-call | flops 8000000000 | bytes 1048576 | tf_op jit(solution)/shard_map/tiles1/pallas_call | solution.py:376
  31.7 0.0 collective-permute-done.4.refs_0_
  31.7 17.3 %tiles2.1 = (f32[3,4096]{1,0:T(4,128)S(1)}, f32[8,8,128]{2,1,0:T(8,128)S(1)}) custom-call(s32[8]{0:T(128)S(1)} %copy-done.7, s32[8]{0:T(128)S(1)} %copy-done.6, s32[8]{0:T(128)S(1)} %copy-done.8, s32[8]{0:T(128)S(1)} %copy-done.9, bf16[4096,128]{1,0:T(8,128)(2,1)S(1)} %copy-done, bf16[3,4096]{1,0:T(4,128)(2,1)S(1)} %copy-done.1, ...), custom_call_target="tpu_custom_call" | custom-call | flops 16000000000 | bytes 1048576 | tf_op jit(solution)/shard_map/tiles2/pallas_call | solution.py:376
  49.0 15.0 %collective-permute-start.7 = (f32[3,4096]{1,0:T(4,128)S(1)}, f32[3,4096]{1,0:T(4,128)S(1)}, u32[]{:S(2)}, u32[]{:S(2)}) collective-permute-start(f32[3,4096]{1,0:T(4,128)S(1)} %get-tuple-element.14), channel_id=1, source_target_pairs={{0,7},{1,0},{2,1},{3,2},{4,3},{5,4},{6,5},{7,6},{8,15},{9,8},{10,9... | collective-permute-start | bytes 147464 | tf_op jit(solution)/shard_map/ppermute | solution.py:25
  63.9 0.0 collective-permute-start.6
  63.9 2.6 %collective-permute-start.5 = (f32[8,8,128]{2,1,0:T(8,128)S(1)}, f32[8,8,128]{2,1,0:T(8,128)S(1)}, u32[]{:S(2)}, u32[]{:S(2)}) collective-permute-start(f32[8,8,128]{2,1,0:T(8,128)S(1)} %get-tuple-element.12), channel_id=1, source_target_pairs={{0,24},{8,0},{16,8},{24,16},{1,25},{9,1},{17,9},{25,17},{2,26},{10... | collective-permute-start | bytes 98312 | tf_op jit(solution)/shard_map/ppermute | solution.py:27
  66.5 2.1 %collective-permute-done.6.corner = f32[8,8,128]{2,1,0:T(8,128)S(1)} collective-permute-done((f32[8,8,128]{2,1,0:T(8,128)S(1)}, f32[8,8,128]{2,1,0:T(8,128)S(1)}, u32[]{:S(2)}, u32[]{:S(2)}) %collective-permute-start.6) | collective-permute-done | bytes 32800 | tf_op jit(solution)/shard_map/ppermute | solution.py:33
  68.6 0.6 collective-permute-done.5.upper
  69.2 0.0 collective-permute-done.7.side
  69.2 1.4 %last.1 = f32[3,4096]{1,0:T(4,128)} custom-call(s32[8]{0:T(128)S(1)} %collective-permute-done.wanted, s32[8]{0:T(128)S(1)} %collective-permute-done.1._.wanted_far, f32[3,4096]{1,0:T(4,128)S(1)} %get-tuple-element.11.total, f32[8,8,128]{2,1,0:T(8,128)S(1)} %collective-permute-done.5.upper, f32[8,8,128]{2,1,0:T(8,128)S(1)} %collective-permute-done.6.corner, ...), custom_call_target="tpu_custom_call" | custom-call | flops 1000000000 | bytes 1048576 | tf_op jit(solution)/shard_map/last/pallas_call | solution.py:376
Async XLA Ops:
  0.0 17.8 %collective-permute-start.2 = (bf16[4096,128]{1,0:T(8,128)(2,1)}, bf16[4096,128]{1,0:T(8,128)(2,1)S(1)}, u32[]{:S(2)}, u32[]{:S(2)}) collective-permute-start(bf16[4096,128]{1,0:T(8,128)(2,1)} %own_f.7), channel_id=1, source_target_pairs={{0,1},{1,2},{2,3},{3,4},{4,5},{5,6},{6,7},{7,0},{8,9},{9,10},{10,1... | collective-permute-start | bytes 3145736 | tf_op jit(solution)/shard_map/ppermute | solution.py:25
  0.5 17.3 %collective-permute-start.1 = (s32[8]{0:T(128)}, s32[8]{0:T(128)S(1)}, u32[]{:S(2)}, u32[]{:S(2)}) collective-permute-start(s32[8]{0:T(128)} %second.5), channel_id=1, source_target_pairs={{0,31},{1,24},{2,25},{3,26},{4,27},{5,28},{6,29},{7,30},{8,7},{9,0... | collective-permute-start | bytes 104 | tf_op jit(solution)/shard_map/ppermute | solution.py:33
  6.9 10.9 %collective-permute-start = (s32[8]{0:T(128)}, s32[8]{0:T(128)S(1)}, u32[]{:S(2)}, u32[]{:S(2)}) collective-permute-start(s32[8]{0:T(128)} %second.5), channel_id=1, source_target_pairs={{0,24},{8,0},{16,8},{24,16},{1,25},{9,1},{17,9},{25,17},{2,26},{10... | collective-permute-start | bytes 104 | tf_op jit(solution)/shard_map/ppermute | solution.py:27
  7.4 10.3 %collective-permute-start.3 = (bf16[3,4096]{1,0:T(4,128)(2,1)}, bf16[3,4096]{1,0:T(4,128)(2,1)S(1)}, u32[]{:S(2)}, u32[]{:S(2)}) collective-permute-start(bf16[3,4096]{1,0:T(4,128)(2,1)} %own_p.7), channel_id=1, source_target_pairs={{0,1},{1,2},{2,3},{3,4},{4,5},{5,6},{6,7},{7,0},{8,9},{9,10},{10,1... | collective-permute-start | bytes 73736 | tf_op jit(solution)/shard_map/ppermute | solution.py:25
  7.4 10.4 %copy-start = (bf16[4096,128]{1,0:T(8,128)(2,1)S(1)}, bf16[4096,128]{1,0:T(8,128)(2,1)}, u32[]{:S(2)}) copy-start(bf16[4096,128]{1,0:T(8,128)(2,1)} %own_f.7) | copy-start | bytes 3145732
  7.4 10.4 %copy-start.1 = (bf16[3,4096]{1,0:T(4,128)(2,1)S(1)}, bf16[3,4096]{1,0:T(4,128)(2,1)}, u32[]{:S(2)}) copy-start(bf16[3,4096]{1,0:T(4,128)(2,1)} %own_p.7) | copy-start | bytes 73732
  17.6 2.7 %copy-start.2 = (bf16[128,128]{1,0:T(8,128)(2,1)S(1)}, bf16[128,128]{1,0:T(8,128)(2,1)}, u32[]{:S(2)}) copy-start(bf16[128,128]{1,0:T(8,128)(2,1)} %refs_2_.3) | copy-start | bytes 98308
  17.7 2.7 %copy-start.3 = (bf16[128,128]{1,0:T(8,128)(2,1)S(1)}, bf16[128,128]{1,0:T(8,128)(2,1)}, u32[]{:S(2)}) copy-start(bf16[128,128]{1,0:T(8,128)(2,1)} %refs_3_.5) | copy-start | bytes 98308
  17.7 2.7 %copy-start.4 = (bf16[128,128]{1,0:T(8,128)(2,1)S(1)}, bf16[128,128]{1,0:T(8,128)(2,1)}, u32[]{:S(2)}) copy-start(bf16[128,128]{1,0:T(8,128)(2,1)} %refs_5_.3) | copy-start | bytes 98308
  17.7 2.7 %copy-start.5 = (bf16[16,128]{1,0:T(8,128)(2,1)S(1)}, bf16[16,128]{1,0:T(8,128)(2,1)}, u32[]{:S(2)}) copy-start(bf16[16,128]{1,0:T(8,128)(2,1)} %refs_4_.3) | copy-start | bytes 12292
  17.7 2.7 %copy-start.6 = (s32[8]{0:T(128)S(1)}, s32[8]{0:T(128)}, u32[]{:S(2)}) copy-start(s32[8]{0:T(128)} %second.5) | copy-start | bytes 100
  17.7 2.7 %copy-start.7 = (s32[8]{0:T(128)S(1)}, s32[8]{0:T(128)}, u32[]{:S(2)}) copy-start(s32[8]{0:T(128)} %first.5) | copy-start | bytes 100
  17.7 2.7 %copy-start.8 = (s32[8]{0:T(128)S(1)}, s32[8]{0:T(128)}, u32[]{:S(2)}) copy-start(s32[8]{0:T(128)} %live_a.5) | copy-start | bytes 100
  17.7 2.7 %copy-start.9 = (s32[8]{0:T(128)S(1)}, s32[8]{0:T(128)}, u32[]{:S(2)}) copy-start(s32[8]{0:T(128)} %live_b.5) | copy-start | bytes 100
  17.7 2.7 %copy-start.10 = (f32[128]{0:T(128)S(1)}, f32[128]{0:T(128)}, u32[]{:S(2)}) copy-start(f32[128]{0:T(128)} %param.21) | copy-start | bytes 1540
  17.7 2.7 %copy-start.11 = (f32[3,4096]{1,0:T(4,128)S(1)}, f32[3,4096]{1,0:T(4,128)}, u32[]{:S(2)}) copy-start(f32[3,4096]{1,0:T(4,128)} %tiles0.1.refs_2_) | copy-start | bytes 147460
  18.5 13.2 %collective-permute-start.4 = (bf16[1152,128]{1,0:T(8,128)(2,1)S(1)}, bf16[1152,128]{1,0:T(8,128)(2,1)S(1)}, u32[]{:S(2)}, u32[]{:S(2)}) collective-permute-start(bf16[1152,128]{1,0:T(8,128)(2,1)S(1)} %pack.1), channel_id=1, source_target_pairs={{0,8},{8,16},{16,24},{24,0},{1,9},{9,17},{17,25},{25,1},{2,10},{10... | collective-permute-start | bytes 884744 | tf_op jit(solution)/shard_map/ppermute | solution.py:27
  49.0 20.2 %collective-permute-start.7 = (f32[3,4096]{1,0:T(4,128)S(1)}, f32[3,4096]{1,0:T(4,128)S(1)}, u32[]{:S(2)}, u32[]{:S(2)}) collective-permute-start(f32[3,4096]{1,0:T(4,128)S(1)} %get-tuple-element.14), channel_id=1, source_target_pairs={{0,7},{1,0},{2,1},{3,2},{4,3},{5,4},{6,5},{7,6},{8,15},{9,8},{10,9... | collective-permute-start | bytes 147464 | tf_op jit(solution)/shard_map/ppermute | solution.py:25
  63.9 4.7 %collective-permute-start.6 = (f32[8,8,128]{2,1,0:T(8,128)S(1)}, f32[8,8,128]{2,1,0:T(8,128)S(1)}, u32[]{:S(2)}, u32[]{:S(2)}) collective-permute-start(f32[8,8,128]{2,1,0:T(8,128)S(1)} %get-tuple-element.12), channel_id=1, source_target_pairs={{0,31},{1,24},{2,25},{3,26},{4,27},{5,28},{6,29},{7,30},{8,7},{9,0... | collective-permute-start | bytes 98312 | tf_op jit(solution)/shard_map/ppermute | solution.py:33
  63.9 5.3 %collective-permute-start.5 = (f32[8,8,128]{2,1,0:T(8,128)S(1)}, f32[8,8,128]{2,1,0:T(8,128)S(1)}, u32[]{:S(2)}, u32[]{:S(2)}) collective-permute-start(f32[8,8,128]{2,1,0:T(8,128)S(1)} %get-tuple-element.12), channel_id=1, source_target_pairs={{0,24},{8,0},{16,8},{24,16},{1,25},{9,1},{17,9},{25,17},{2,26},{10... | collective-permute-start | bytes 98312 | tf_op jit(solution)/shard_map/ppermute | solution.py:27

commit v2 on v1

--- a/solution.py
+++ b/solution.py
@@ -49,7 +49,7 @@
     return jnp.concatenate([places.astype(F32), jnp.zeros((5, CELL), F32)], axis=0)
 
 
-def pack_kernel(wanted, _, own_f, own_p, side_f, side_p, out):
+def pack_kernel(wanted, own_f, own_p, side_f, side_p, out):
     cells = own_f.shape[0] // CELL
     for slot in range(wanted.shape[0]):
         block, cell = wanted[slot] // cells, wanted[slot] % cells
@@ -357,16 +357,23 @@
     lax.fori_loop(0, picked, finish, 0)
 
 
-def last_kernel(wanted, wanted_far, total, upper, corner, side, out):
+def hand_kernel(wanted, total, side, got, total_out, side_out):
     cells = total.shape[1] // CELL
-    out[...] = -(total[...] + side[...])
+    total_out[...] = total[...]
+    side_out[...] = side[...]
     for slot in range(wanted.shape[0]):
-        for asked, block, got in ((wanted, 2, upper), (wanted_far, 3, corner)):
-
-            @pl.when(asked[slot] // cells == block)
-            def _(asked=asked, got=got, slot=slot):
-                here = pl.ds(pl.multiple_of(asked[slot] % cells * CELL, CELL), CELL)
-                out[:, here] = out[:, here] - got[slot][0:3]
+        block = wanted[slot] // cells
+        here = pl.ds(pl.multiple_of(wanted[slot] % cells * CELL, CELL), CELL)
+
+        def add(sums, slot=slot, here=here):
+            sums[:, here] = sums[:, here] + got[slot][0:3]
+
+        pl.when(block == 2)(functools.partial(add, total_out))
+        pl.when(block == 3)(functools.partial(add, side_out))
+
+
+def last_kernel(total, got, out):
+    out[...] = -(total[...] + got[...])
 
 
 def called(kernel, prefetch, operands, out_shape, scratch=(), work=1.0, name=None, bring=False):
@@ -407,7 +414,6 @@
     side_f = shifted(features, 0, 1)
     side_p = shifted(positions, 0, 1)
     asked = shifted(tile_second, -1, 0)
-    asked_far = shifted(tile_second, -1, -1)
 
     scalars = (tile_first, tile_second, count_first, count_second)
     weights = (w_first, w_second, radial_weight, mix_weight, out_weight.reshape(1, -1))
@@ -440,7 +446,7 @@
     (total,) = tiles(0, (), (sums,), 8.0)
     packed = called(
         pack_kernel,
-        (asked, asked_far),
+        (asked,),
         (features, positions, side_f, side_p),
         jax.ShapeDtypeStruct((count * PACKED, CELL), BF),
         name="pack",
@@ -450,12 +456,9 @@
     grads = jax.ShapeDtypeStruct((count, 8, CELL), F32)
     total, grads = tiles(2, (upper_cells, total), (sums, grads), 16.0)
     from_upper = shifted(grads, -1, 0)
-    from_corner = shifted(grads, -1, -1)
-    side, _ = lax.optimization_barrier((side, grads))
+    total, side = called(hand_kernel, (asked,), (total, side, from_upper), (sums, sums), name="hand")
     from_side = shifted(side, 0, -1)
-    return called(
-        last_kernel, (asked, asked_far), (total, from_upper, from_corner, from_side), sums, name="last"
-    )
+    return called(last_kernel, (), (total, from_side), sums, name="last")
 
 
 def solution(mesh):

time: 70.9 us -> 75.2 us (1.061)
  the two profiles are of different devices: /device:TPU:0 before, /device:TPU:1 now
where the time goes in v2:
time: 75.2 us; the launch traced here: 73.9 us
  Pallas kernels  42 us (56%)
  starting transfers between devices  26.8 us (36%)
  waiting for transfers between devices  4.71 us (6%)
    pallas_call x6, Pallas kernels, called(): pl.pallas_call(kernel, grid_spec=pltpu.PrefetchScalarGridSpec(num_scalar_...  42 us
    ppermute x3, starting transfers between devices, shifted(): lax.ppermute(array, 'grp', [(i, (i + groups) % n_grp) for i in range(n_gr...  23.8 us
    ppermute x3, waiting for transfers between devices, shifted(): lax.ppermute(array, 'dev', [(i, (i + members) % n_dev) for i in range(n_d...  3.68 us
    ppermute x3, starting transfers between devices, shifted(): lax.ppermute(array, 'dev', [(i, (i + members) % n_dev) for i in range(n_d...  3.02 us
  transfers between devices with their start and end apart: 6, of which 2 were waited for; matrix products, arithmetic and copies ran while one was open for 0% of the time, Pallas kernels for 38%

profile of v2, /device:TPU:1, one launch (start us, length us, event | category | flops | bytes accessed | tf_op | source)
XLA Modules:
  0.0 73.9 jit_solution(1726472754282314655)
XLA Ops:
  0.0 2.7 %collective-permute-start.1 = (bf16[4096,128]{1,0:T(8,128)(2,1)}, bf16[4096,128]{1,0:T(8,128)(2,1)S(1)}, u32[]{:S(2)}, u32[]{:S(2)}) collective-permute-start(bf16[4096,128]{1,0:T(8,128)(2,1)} %own_f.7), channel_id=1, source_target_pairs={{0,1},{1,2},{2,3},{3,4},{4,5},{5,6},{6,7},{7,0},{8,9},{9,10},{10,1... | collective-permute-start | bytes 3145736 | tf_op jit(solution)/shard_map/ppermute | solution.py:25
  2.7 2.2 %collective-permute-start = (s32[8]{0:T(128)}, s32[8]{0:T(128)S(1)}, u32[]{:S(2)}, u32[]{:S(2)}) collective-permute-start(s32[8]{0:T(128)} %second.5), channel_id=1, source_target_pairs={{0,24},{8,0},{16,8},{24,16},{1,25},{9,1},{17,9},{25,17},{2,26},{10... | collective-permute-start | bytes 104 | tf_op jit(solution)/shard_map/ppermute | solution.py:27
  4.8 0.3 collective-permute-start.2
  5.1 0.0 copy-start
  5.1 0.0 copy-start.1
  5.1 12.8 %tiles0.1.refs_2_ = f32[3,4096]{1,0:T(4,128)} custom-call(s32[8]{0:T(128)} %first.5, s32[8]{0:T(128)} %second.5, s32[8]{0:T(128)} %live_a.5, s32[8]{0:T(128)} %live_b.5, bf16[4096,128]{1,0:T(8,128)(2,1)} %own_f.7, bf16[3,4096]{1,0:T(4,128)(2,1)} %own_p.7, bf16[128,128]{1,0:T(8,128)(2,1)} %refs_2_.3, bf16[128,128]{1,0:T(8,128)(2,1)} %refs_3_.5, ...), custom_call_target="tpu_custom_call" | custom-call | flops 8000000000 | bytes 1048576 | tf_op jit(solution)/shard_map/tiles0/pallas_call | solution.py:383
  18.0 0.0 copy-start.2
  18.0 0.0 copy-start.3
  18.0 0.0 copy-start.4
  18.0 0.0 copy-start.5
  18.0 0.0 copy-start.6
  18.0 0.0 copy-start.7
  18.0 0.0 copy-start.8
  18.0 0.0 copy-start.9
  18.0 0.0 copy-start.10
  18.1 0.0 copy-start.11
  18.1 0.0 collective-permute-done.wanted
  18.1 0.0 collective-permute-done.2.side_p.refs_1_
  18.1 0.0 collective-permute-done.1.side_f.refs_0_
  18.1 0.0 copy-done
  18.1 0.0 copy-done.1
  18.1 0.7 pack.1
  18.8 0.1 collective-permute-start.3
  18.9 0.0 copy-done.2
  18.9 0.0 copy-done.3
  18.9 0.0 copy-done.4
  18.9 0.0 copy-done.5
  18.9 0.0 copy-done.6
  19.0 0.0 copy-done.7
  19.0 0.0 copy-done.8
  19.0 0.0 copy-done.9
  19.0 0.0 copy-done.10
  19.0 0.0 copy-done.11
  19.0 15.2 %tiles1.1 = (f32[3,4096]{1,0:T(4,128)S(1)}, f32[3,4096]{1,0:T(4,128)S(1)}) custom-call(s32[8]{0:T(128)S(1)} %copy-done.7, s32[8]{0:T(128)S(1)} %copy-done.6, s32[8]{0:T(128)S(1)} %copy-done.8, s32[8]{0:T(128)S(1)} %copy-done.9, bf16[4096,128]{1,0:T(8,128)(2,1)S(1)} %copy-done, bf16[3,4096]{1,0:T(4,128)(2,1)S(1)} %copy-done.1, ...), custom_call_target="tpu_custom_call" | custom-call | flops 8000000000 | bytes 1048576 | tf_op jit(solution)/shard_map/tiles1/pallas_call | solution.py:383
  34.3 0.0 collective-permute-done.3.refs_0_
  34.3 11.9 %tiles2.1 = (f32[3,4096]{1,0:T(4,128)S(1)}, f32[8,8,128]{2,1,0:T(8,128)S(1)}) custom-call(s32[8]{0:T(128)S(1)} %copy-done.7, s32[8]{0:T(128)S(1)} %copy-done.6, s32[8]{0:T(128)S(1)} %copy-done.8, s32[8]{0:T(128)S(1)} %copy-done.9, bf16[4096,128]{1,0:T(8,128)(2,1)S(1)} %copy-done, bf16[3,4096]{1,0:T(4,128)(2,1)S(1)} %copy-done.1, ...), custom_call_target="tpu_custom_call" | custom-call | flops 16000000000 | bytes 1048576 | tf_op jit(solution)/shard_map/tiles2/pallas_call | solution.py:383
  46.2 21.6 %collective-permute-start.4 = (f32[8,8,128]{2,1,0:T(8,128)S(1)}, f32[8,8,128]{2,1,0:T(8,128)S(1)}, u32[]{:S(2)}, u32[]{:S(2)}) collective-permute-start(f32[8,8,128]{2,1,0:T(8,128)S(1)} %get-tuple-element.14), channel_id=1, source_target_pairs={{0,24},{8,0},{16,8},{24,16},{1,25},{9,1},{17,9},{25,17},{2,26},{10... | collective-permute-start | bytes 98312 | tf_op jit(solution)/shard_map/ppermute | solution.py:27
  67.8 1.0 %collective-permute-done.4.got = f32[8,8,128]{2,1,0:T(8,128)S(1)} collective-permute-done((f32[8,8,128]{2,1,0:T(8,128)S(1)}, f32[8,8,128]{2,1,0:T(8,128)S(1)}, u32[]{:S(2)}, u32[]{:S(2)}) %collective-permute-start.4) | collective-permute-done | bytes 32800 | tf_op jit(solution)/shard_map/ppermute | solution.py:27
  68.8 0.7 hand.1
  69.5 0.1 collective-permute-start.5
  69.6 3.7 %collective-permute-done.5.got = f32[3,4096]{1,0:T(4,128)S(1)} collective-permute-done((f32[3,4096]{1,0:T(4,128)S(1)}, f32[3,4096]{1,0:T(4,128)S(1)}, u32[]{:S(2)}, u32[]{:S(2)}) %collective-permute-start.5) | collective-permute-done | bytes 49184 | tf_op jit(solution)/shard_map/ppermute | solution.py:25
  73.2 0.6 last.1
Async XLA Ops:
  0.0 18.1 %collective-permute-start.1 = (bf16[4096,128]{1,0:T(8,128)(2,1)}, bf16[4096,128]{1,0:T(8,128)(2,1)S(1)}, u32[]{:S(2)}, u32[]{:S(2)}) collective-permute-start(bf16[4096,128]{1,0:T(8,128)(2,1)} %own_f.7), channel_id=1, source_target_pairs={{0,1},{1,2},{2,3},{3,4},{4,5},{5,6},{6,7},{7,0},{8,9},{9,10},{10,1... | collective-permute-start | bytes 3145736 | tf_op jit(solution)/shard_map/ppermute | solution.py:25
  2.7 15.4 %collective-permute-start = (s32[8]{0:T(128)}, s32[8]{0:T(128)S(1)}, u32[]{:S(2)}, u32[]{:S(2)}) collective-permute-start(s32[8]{0:T(128)} %second.5), channel_id=1, source_target_pairs={{0,24},{8,0},{16,8},{24,16},{1,25},{9,1},{17,9},{25,17},{2,26},{10... | collective-permute-start | bytes 104 | tf_op jit(solution)/shard_map/ppermute | solution.py:27
  4.8 13.2 %collective-permute-start.2 = (bf16[3,4096]{1,0:T(4,128)(2,1)}, bf16[3,4096]{1,0:T(4,128)(2,1)S(1)}, u32[]{:S(2)}, u32[]{:S(2)}) collective-permute-start(bf16[3,4096]{1,0:T(4,128)(2,1)} %own_p.7), channel_id=1, source_target_pairs={{0,1},{1,2},{2,3},{3,4},{4,5},{5,6},{6,7},{7,0},{8,9},{9,10},{10,1... | collective-permute-start | bytes 73736 | tf_op jit(solution)/shard_map/ppermute | solution.py:25
  5.1 13.0 %copy-start = (bf16[4096,128]{1,0:T(8,128)(2,1)S(1)}, bf16[4096,128]{1,0:T(8,128)(2,1)}, u32[]{:S(2)}) copy-start(bf16[4096,128]{1,0:T(8,128)(2,1)} %own_f.7) | copy-start | bytes 3145732
  5.1 13.0 %copy-start.1 = (bf16[3,4096]{1,0:T(4,128)(2,1)S(1)}, bf16[3,4096]{1,0:T(4,128)(2,1)}, u32[]{:S(2)}) copy-start(bf16[3,4096]{1,0:T(4,128)(2,1)} %own_p.7) | copy-start | bytes 73732
  18.0 1.0 %copy-start.2 = (bf16[128,128]{1,0:T(8,128)(2,1)S(1)}, bf16[128,128]{1,0:T(8,128)(2,1)}, u32[]{:S(2)}) copy-start(bf16[128,128]{1,0:T(8,128)(2,1)} %refs_2_.3) | copy-start | bytes 98308
  18.0 1.0 %copy-start.3 = (bf16[128,128]{1,0:T(8,128)(2,1)S(1)}, bf16[128,128]{1,0:T(8,128)(2,1)}, u32[]{:S(2)}) copy-start(bf16[128,128]{1,0:T(8,128)(2,1)} %refs_3_.5) | copy-start | bytes 98308
  18.0 1.0 %copy-start.4 = (bf16[128,128]{1,0:T(8,128)(2,1)S(1)}, bf16[128,128]{1,0:T(8,128)(2,1)}, u32[]{:S(2)}) copy-start(bf16[128,128]{1,0:T(8,128)(2,1)} %refs_5_.3) | copy-start | bytes 98308
  18.0 1.0 %copy-start.5 = (bf16[16,128]{1,0:T(8,128)(2,1)S(1)}, bf16[16,128]{1,0:T(8,128)(2,1)}, u32[]{:S(2)}) copy-start(bf16[16,128]{1,0:T(8,128)(2,1)} %refs_4_.3) | copy-start | bytes 12292
  18.0 1.0 %copy-start.6 = (s32[8]{0:T(128)S(1)}, s32[8]{0:T(128)}, u32[]{:S(2)}) copy-start(s32[8]{0:T(128)} %second.5) | copy-start | bytes 100
  18.0 0.9 %copy-start.7 = (s32[8]{0:T(128)S(1)}, s32[8]{0:T(128)}, u32[]{:S(2)}) copy-start(s32[8]{0:T(128)} %first.5) | copy-start | bytes 100
  18.0 0.9 %copy-start.8 = (s32[8]{0:T(128)S(1)}, s32[8]{0:T(128)}, u32[]{:S(2)}) copy-start(s32[8]{0:T(128)} %live_a.5) | copy-start | bytes 100
  18.0 0.9 %copy-start.9 = (s32[8]{0:T(128)S(1)}, s32[8]{0:T(128)}, u32[]{:S(2)}) copy-start(s32[8]{0:T(128)} %live_b.5) | copy-start | bytes 100
  18.0 0.9 %copy-start.10 = (f32[128]{0:T(128)S(1)}, f32[128]{0:T(128)}, u32[]{:S(2)}) copy-start(f32[128]{0:T(128)} %param.21) | copy-start | bytes 1540
  18.1 0.9 %copy-start.11 = (f32[3,4096]{1,0:T(4,128)S(1)}, f32[3,4096]{1,0:T(4,128)}, u32[]{:S(2)}) copy-start(f32[3,4096]{1,0:T(4,128)} %tiles0.1.refs_2_) | copy-start | bytes 147460
  18.8 15.4 %collective-permute-start.3 = (bf16[1152,128]{1,0:T(8,128)(2,1)S(1)}, bf16[1152,128]{1,0:T(8,128)(2,1)S(1)}, u32[]{:S(2)}, u32[]{:S(2)}) collective-permute-start(bf16[1152,128]{1,0:T(8,128)(2,1)S(1)} %pack.1), channel_id=1, source_target_pairs={{0,8},{8,16},{16,24},{24,0},{1,9},{9,17},{17,25},{25,1},{2,10},{10... | collective-permute-start | bytes 884744 | tf_op jit(solution)/shard_map/ppermute | solution.py:27
  46.2 22.6 %collective-permute-start.4 = (f32[8,8,128]{2,1,0:T(8,128)S(1)}, f32[8,8,128]{2,1,0:T(8,128)S(1)}, u32[]{:S(2)}, u32[]{:S(2)}) collective-permute-start(f32[8,8,128]{2,1,0:T(8,128)S(1)} %get-tuple-element.14), channel_id=1, source_target_pairs={{0,24},{8,0},{16,8},{24,16},{1,25},{9,1},{17,9},{25,17},{2,26},{10... | collective-permute-start | bytes 98312 | tf_op jit(solution)/shard_map/ppermute | solution.py:27
  69.5 3.7 %collective-permute-start.5 = (f32[3,4096]{1,0:T(4,128)S(1)}, f32[3,4096]{1,0:T(4,128)S(1)}, u32[]{:S(2)}, u32[]{:S(2)}) collective-permute-start(f32[3,4096]{1,0:T(4,128)S(1)} %get-tuple-element.16), channel_id=1, source_target_pairs={{0,7},{1,0},{2,1},{3,2},{4,3},{5,4},{6,5},{7,6},{8,15},{9,8},{10,9... | collective-permute-start | bytes 147464 | tf_op jit(solution)/shard_map/ppermute | solution.py:25
